TPU v7x, 768 devices: a whole 4x8x12 slice. The times are simulated.
768 devices in a mesh: dp: 32 (over x, y), expert: 24 (over z, core).
Axes of the slice: x: 4, y: 8, z: 12, core: 2. Of those that a mesh axis runs over, the one named last changes fastest.
Arguments:
- tokens: bfloat16 [98304, 2048], P(('dp', 'expert')), may hold values from -6 to 6
- routes: int32 [98304, 2], P(('dp', 'expert')), may hold values from 0 to 23, all different within a row; in each aligned block of 128 rows (0 to 127, 128 to 255, ...) at most 11 rows name the same one
- route_scores: float32 [98304, 2], P(('dp', 'expert')), may hold values from -4 to 4
- out_grad: bfloat16 [98304, 2048], P(('dp', 'expert')), may hold values from -6 to 6
- gate_up: bfloat16 [24, 2048, 1024], P('expert'), may hold values from -0.125 to 0.125
- down_weight: bfloat16 [24, 2048, 512], P('expert'), may hold values from -0.25 to 0.25
Outputs:
- mixed_out: bfloat16 [98304, 2048], P(('dp', 'expert'))
- token_grad: bfloat16 [98304, 2048], P(('dp', 'expert'))
- grad_gate_up: float32 [24, 2048, 1024], P('expert', 'dp')
- grad_down: float32 [24, 2048, 512], P('expert', 'dp')
Inputs may be any that keep to these rules, and one draw needn't show every extreme that they name: `routes`: the 2 experts of a token differ. Among the 128 tokens of one device no expert is named more than 11 times, and in some device's tokens an expert is named exactly 11 times.
All inputs are finite; a program needn't handle non-finite values.
Results may differ from a plain program's by a relative error of at most 0.015.
Values may be sent and summed in bfloat16 or wider, within the bound.
A program may use at most 64 MiB of HBM per device.

v0:
```python
import jax
import jax.numpy as jnp
from jax import lax
from jax.sharding import PartitionSpec as P


def contract(left, right):
    return lax.dot_general(
        left, right, (((0,), (0,)), ((), ())), preferred_element_type=jnp.float32
    )


def expert_forward(row_block, w_in, w_out):
    model_width = row_block.shape[-1]
    hidden_units = w_out.shape[1]
    leading = row_block.shape[:-1]
    flat_rows = row_block.reshape(-1, model_width)
    preact = jnp.dot(flat_rows, w_in, preferred_element_type=jnp.float32)
    gate_pre = preact[:, :hidden_units]
    up_pre = preact[:, hidden_units:]
    hidden = (jax.nn.silu(gate_pre) * up_pre).astype(jnp.bfloat16)
    produced = jnp.dot(hidden, w_out.T, preferred_element_type=jnp.float32).astype(jnp.bfloat16)
    return (
        produced.reshape(leading + (model_width,)),
        preact.reshape(leading + (2 * hidden_units,)),
        hidden.reshape(leading + (hidden_units,)),
    )


def expert_backward(grad_block, preact, w_in, w_out):
    model_width = w_out.shape[0]
    hidden_units = w_out.shape[1]
    leading = grad_block.shape[:-1]
    grad_rows = grad_block.reshape(-1, model_width)
    pre_rows = preact.reshape(-1, 2 * hidden_units)
    gate_pre = pre_rows[:, :hidden_units]
    up_pre = pre_rows[:, hidden_units:]
    hidden_grad = jnp.dot(grad_rows, w_out, preferred_element_type=jnp.float32)
    sigmoid_gate = jax.nn.sigmoid(gate_pre)
    gate_grad = hidden_grad * up_pre * sigmoid_gate * (1.0 + gate_pre * (1.0 - sigmoid_gate))
    up_grad = hidden_grad * gate_pre * sigmoid_gate
    pre_grad = jnp.concatenate([gate_grad, up_grad], axis=1).astype(jnp.bfloat16)
    input_grad = jnp.dot(pre_grad, w_in.T, preferred_element_type=jnp.float32).astype(jnp.bfloat16)
    return (
        pre_grad.reshape(leading + (2 * hidden_units,)),
        input_grad.reshape(leading + (model_width,)),
    )


def whole_share(token_rows, pre_grad_rows, grad_rows, hidden_rows):
    return lax.psum_scatter(
        jnp.concatenate(
            [contract(token_rows, pre_grad_rows), contract(grad_rows, hidden_rows)], axis=1
        ).astype(jnp.bfloat16),
        "dp",
        scatter_dimension=0,
        tiled=True,
    ).astype(jnp.float32)


def body(tokens, routes, route_scores, out_grad, gate_up, down_weight):
    expert_count = lax.axis_size("expert")
    group_count = lax.axis_size("dp")
    tok_rows, model_width = tokens.shape
    top_count = routes.shape[1]
    hidden_units = down_weight.shape[2]
    capacity = (tok_rows * top_count + expert_count - 1) // expert_count
    slot_count = expert_count * capacity
    route_count = tok_rows * top_count
    share_rows = model_width // group_count
    w_in = gate_up[0]
    w_out = down_weight[0]
    flat_routes = routes.reshape(route_count)
    expert_ids = lax.broadcasted_iota(jnp.int32, (route_count, expert_count), 1)
    chosen = (flat_routes[:, None] == expert_ids).astype(jnp.int32)
    position = jnp.sum((jnp.cumsum(chosen, axis=0) - chosen) * chosen, axis=1)
    slot_index = flat_routes * capacity + position
    slot_source = jnp.full((slot_count,), route_count, jnp.int32)
    slot_source = slot_source.at[slot_index].set(jnp.arange(route_count, dtype=jnp.int32))
    scores_exp = jnp.exp(route_scores)
    weights = scores_exp / jnp.sum(scores_exp, axis=1, keepdims=True)
    zero_row = jnp.zeros((1, model_width), jnp.bfloat16)
    rows_source = jnp.concatenate([jnp.repeat(tokens, top_count, axis=0), zero_row], axis=0)
    sent_rows = rows_source[slot_source].reshape(expert_count, capacity, model_width)
    route_grad = (weights[:, :, None] * out_grad[:, None, :].astype(jnp.float32)).astype(
        jnp.bfloat16
    )
    grads_source = jnp.concatenate([route_grad.reshape(route_count, model_width), zero_row], axis=0)
    sent_grads = grads_source[slot_source].reshape(expert_count, capacity, model_width)
    down_sum = None
    received = lax.all_to_all(sent_rows, "expert", split_axis=0, concat_axis=0, tiled=True)
    produced, preact, hidden = expert_forward(received, w_in, w_out)
    returned = lax.all_to_all(produced, "expert", split_axis=0, concat_axis=0, tiled=True)
    got_grads = lax.all_to_all(sent_grads, "expert", split_axis=0, concat_axis=0, tiled=True)
    grad_rows = got_grads.reshape(slot_count, model_width)
    hidden_rows = hidden.reshape(slot_count, hidden_units)
    pre_grad, input_grad = expert_backward(got_grads, preact, w_in, w_out)
    sent_back = lax.all_to_all(input_grad, "expert", split_axis=0, concat_axis=0, tiled=True)
    token_rows = received.reshape(slot_count, model_width)
    pre_grad_rows = pre_grad.reshape(slot_count, 2 * hidden_units)
    summed = whole_share(token_rows, pre_grad_rows, grad_rows, hidden_rows)
    input_sum = summed[:, : 2 * hidden_units]
    down_sum = summed[:, 2 * hidden_units :]
    picked = (
        returned.reshape(slot_count, model_width)[slot_index]
        .astype(jnp.float32)
        .reshape(tok_rows, top_count, model_width)
    )
    mixed_out = jnp.sum(weights[:, :, None] * picked, axis=1).astype(jnp.bfloat16)
    back_grads = (
        sent_back.reshape(slot_count, model_width)[slot_index]
        .astype(jnp.float32)
        .reshape(tok_rows, top_count, model_width)
    )
    token_grad = jnp.sum(back_grads, axis=1).astype(jnp.bfloat16)
    grad_gate_up = (input_sum / group_count).reshape(1, share_rows, 2 * hidden_units)
    grad_down = (down_sum / group_count).reshape(1, share_rows, hidden_units)
    return (mixed_out, token_grad, grad_gate_up, grad_down)


def solution(mesh):
    in_specs = (
        P(("dp", "expert"), None),
        P(("dp", "expert"), None),
        P(("dp", "expert"), None),
        P(("dp", "expert"), None),
        P("expert", None, None),
        P("expert", None, None),
    )
    out_specs = (
        P(("dp", "expert"), None),
        P(("dp", "expert"), None),
        P("expert", "dp", None),
        P("expert", "dp", None),
    )
    return jax.shard_map(body, mesh=mesh, in_specs=in_specs, out_specs=out_specs, check_vma=False)
```

profile of v0, /device:TPU:1, one launch (start us, length us, event | category | flops | bytes accessed | tf_op | source)
XLA Modules:
  0.0 417.2 jit_solution(12810361527143236759)
XLA Ops:
  7.2 0.9 copy.23
  8.4 0.7 broadcast_multiply_fusion
  9.1 0.6 reduce-window.6
  9.7 0.2 slice_reduce_fusion
  10.3 1.4 scatter_custom_fusion
  11.7 1.7 broadcast_in_dim.6
  13.4 1.2 reshape.100
  14.6 1.3 concatenate.14
  15.9 2.9 gather_fusion
  18.8 2.6 reshape.102
  21.4 16.8 %all-to-all-start = ((bf16[24,11,2048]{2,1,0:T(8,128)(2,1)}), bf16[24,11,2048]{2,1,0:T(8,128)(2,1)}, u32[]{:S(2)}, u32[]{:S(2)}) async-start(bf16[24,11,2048]{2,1,0:T(8,128)(2,1)} %reshape.102), calls=%async_computation | async-start | bytes 3145728 | tf_op jit(solution)/shard_map/all_to_all | solution.py:91
  38.6 2.4 mul.80
  41.0 3.7 mul.81
  44.6 1.8 multiply_convert_fusion
  46.5 2.9 gather_fusion.2
  49.5 2.5 reshape.106
  52.0 42.6 %all-to-all-done = bf16[24,11,2048]{2,1,0:T(8,128)(2,1)} async-done(((bf16[24,11,2048]{2,1,0:T(8,128)(2,1)}), bf16[24,11,2048]{2,1,0:T(8,128)(2,1)}, u32[]{:S(2)}, u32[]{:S(2)}) %all-to-all-start) | async-done | bytes 1081376 | tf_op jit(solution)/shard_map/all_to_all | solution.py:91
  94.6 6.0 %all-to-all-start.2 = ((bf16[24,11,2048]{2,1,0:T(8,128)(2,1)}), bf16[24,11,2048]{2,1,0:T(8,128)(2,1)}, u32[]{:S(2)}, u32[]{:S(2)}) async-start(bf16[24,11,2048]{2,1,0:T(8,128)(2,1)} %reshape.106), calls=%async_computation.2 | async-start | bytes 3145728 | tf_op jit(solution)/shard_map/all_to_all | solution.py:94
  100.6 0.2 reduce-scatter.4.cloned.1.call-start
  100.8 1.7 reshape.103
  102.5 4.5 %fusion.2 = f32[264,1024]{1,0:T(8,128)} fusion(bf16[264,2048]{1,0:T(8,128)(2,1)S(1)} %reshape.103, bf16[1,2048,1024]{2,1,0:T(8,128)(2,1)} %param.10), kind=kOutput, calls=%fused_computation.8 | convolution fusion | flops 1107296256 | bytes 6356992 | tf_op jit(solution)/shard_map/dot_general | solution.py:18
  107.0 50.1 %all-to-all-done.2 = bf16[24,11,2048]{2,1,0:T(8,128)(2,1)} async-done(((bf16[24,11,2048]{2,1,0:T(8,128)(2,1)}), bf16[24,11,2048]{2,1,0:T(8,128)(2,1)}, u32[]{:S(2)}, u32[]{:S(2)}) %all-to-all-start.2) | async-done | bytes 1081376 | tf_op jit(solution)/shard_map/all_to_all | solution.py:94
  157.1 2.5 reshape.107
  159.6 2.5 multiply_convert_fusion.2
  162.2 1.3 convolution_convert_fusion.1
  163.5 2.4 convolution_convert_fusion
  165.9 3.5 pad_maximum_fusion
  169.4 8.7 %copy.29 = bf16[2048,1536]{1,0:T(8,128)(2,1)} copy(bf16[2048,1536]{0,1:T(8,128)(2,1)} %pad_maximum_fusion) | data formatting | bytes 12582912
  178.1 3.7 fusion.4
  181.8 1.6 reshape.108
  183.4 5.8 %all-to-all-start.3 = ((bf16[24,11,2048]{2,1,0:T(8,128)(2,1)}), bf16[24,11,2048]{2,1,0:T(8,128)(2,1)}, u32[]{:S(2)}, u32[]{:S(2)}) async-start(bf16[24,11,2048]{2,1,0:T(8,128)(2,1)} %reshape.108), calls=%async_computation.3 | async-start | bytes 3145728 | tf_op jit(solution)/shard_map/all_to_all | solution.py:98
  189.2 0.8 convolution_convert_fusion.2
  190.0 1.5 reshape.104
  191.5 54.2 %all-to-all-done.3 = bf16[24,11,2048]{2,1,0:T(8,128)(2,1)} async-done(((bf16[24,11,2048]{2,1,0:T(8,128)(2,1)}), bf16[24,11,2048]{2,1,0:T(8,128)(2,1)}, u32[]{:S(2)}, u32[]{:S(2)}) %all-to-all-start.3) | async-done | bytes 1081376 | tf_op jit(solution)/shard_map/all_to_all | solution.py:98
  245.7 5.8 %all-to-all-start.1 = ((bf16[24,11,2048]{2,1,0:T(8,128)(2,1)}), bf16[24,11,2048]{2,1,0:T(8,128)(2,1)}, u32[]{:S(2)}, u32[]{:S(2)}) async-start(bf16[24,11,2048]{2,1,0:T(8,128)(2,1)} %reshape.104), calls=%async_computation.1 | async-start | bytes 3145728 | tf_op jit(solution)/shard_map/all_to_all | solution.py:93
  251.6 1.7 reshape.109
  253.3 2.3 gather_fusion.3
  255.6 1.8 gather.18
  257.4 3.6 reduce_sum.45
  261.0 47.0 %all-to-all-done.1 = bf16[24,11,2048]{2,1,0:T(8,128)(2,1)} async-done(((bf16[24,11,2048]{2,1,0:T(8,128)(2,1)}), bf16[24,11,2048]{2,1,0:T(8,128)(2,1)}, u32[]{:S(2)}, u32[]{:S(2)}) %all-to-all-start.1) | async-done | bytes 1081376 | tf_op jit(solution)/shard_map/all_to_all | solution.py:93
  308.0 1.7 reshape.105
  309.7 2.4 gather_fusion.1
  312.2 3.3 reshape.112
  315.5 5.6 %multiply_reduce_fusion = bf16[128,2048]{1,0:T(8,128)(2,1)} fusion(f32[128,2,2048]{2,1,0:T(2,128)} %reshape.112, f32[128,2]{1,0:T(8,128)S(1)} %copy.21), kind=kLoop, calls=%fused_computation.18 | loop fusion | flops 786432 | bytes 2622464 | tf_op jit(solution)/shard_map/reduce_sum | solution.py:109
  321.1 86.4 %reduce-scatter.4.cloned.1.call-done = bf16[64,1536]{1,0:T(8,128)(2,1)} async-done(((bf16[2048,1536]{1,0:T(8,128)(2,1)}), bf16[64,1536]{1,0:T(8,128)(2,1)}) %reduce-scatter.4.cloned.1.call-update) | async-done | bytes 196624
  407.4 1.1 copy.30
  408.7 0.9 copy.27
  409.6 0.8 copy.28
  (34 shorter events, 1.3 us)
Async XLA Ops:
  7.2 152.5 %copy-start = (bf16[1,2048,512]{2,1,0:T(8,128)(2,1)S(1)}, bf16[1,2048,512]{2,1,0:T(8,128)(2,1)}, u32[]{:S(2)}) copy-start(bf16[1,2048,512]{2,1,0:T(8,128)(2,1)} %param.11) | copy-start | bytes 6291460
  21.4 16.9 %copy-start.3 = (f32[128,2]{0,1:T(2,128)S(1)}, f32[128,2]{0,1:T(2,128)}, u32[]{:S(2)}) copy-start(f32[128,2]{0,1:T(2,128)} %param.8) | copy-start | bytes 3076
  21.4 17.2 %copy-start.2 = (bf16[128,2048]{1,0:T(8,128)(2,1)S(1)}, bf16[128,2048]{1,0:T(8,128)(2,1)}, u32[]{:S(2)}) copy-start(bf16[128,2048]{1,0:T(8,128)(2,1)} %param.9) | copy-start | bytes 1572868
  21.4 73.2 %all-to-all-start = ((bf16[24,11,2048]{2,1,0:T(8,128)(2,1)}), bf16[24,11,2048]{2,1,0:T(8,128)(2,1)}, u32[]{:S(2)}, u32[]{:S(2)}) async-start(bf16[24,11,2048]{2,1,0:T(8,128)(2,1)} %reshape.102), calls=%async_computation | async-start | bytes 3145728 | tf_op jit(solution)/shard_map/all_to_all | solution.py:91
  94.6 62.5 %all-to-all-start.2 = ((bf16[24,11,2048]{2,1,0:T(8,128)(2,1)}), bf16[24,11,2048]{2,1,0:T(8,128)(2,1)}, u32[]{:S(2)}, u32[]{:S(2)}) async-start(bf16[24,11,2048]{2,1,0:T(8,128)(2,1)} %reshape.106), calls=%async_computation.2 | async-start | bytes 3145728 | tf_op jit(solution)/shard_map/all_to_all | solution.py:94
  100.6 306.9 %reduce-scatter.4.cloned.1.call-start = ((), (), s32[]{:S(2)}) async-start(), calls=%async_computation.5 | async-start | bytes 6488064
  159.6 2.5 copy-start.1
  162.1 1.4 copy-start.4
  162.2 1.4 copy-start.5
  183.4 62.4 %all-to-all-start.3 = ((bf16[24,11,2048]{2,1,0:T(8,128)(2,1)}), bf16[24,11,2048]{2,1,0:T(8,128)(2,1)}, u32[]{:S(2)}, u32[]{:S(2)}) async-start(bf16[24,11,2048]{2,1,0:T(8,128)(2,1)} %reshape.108), calls=%async_computation.3 | async-start | bytes 3145728 | tf_op jit(solution)/shard_map/all_to_all | solution.py:98
  245.7 62.3 %all-to-all-start.1 = ((bf16[24,11,2048]{2,1,0:T(8,128)(2,1)}), bf16[24,11,2048]{2,1,0:T(8,128)(2,1)}, u32[]{:S(2)}, u32[]{:S(2)}) async-start(bf16[24,11,2048]{2,1,0:T(8,128)(2,1)} %reshape.104), calls=%async_computation.1 | async-start | bytes 3145728 | tf_op jit(solution)/shard_map/all_to_all | solution.py:93
Sparse Core Ops, SparseCore 0:
  178.2 229.2 reduce-scatter.3
where the time goes:
time: 421 us; the launch traced here: 417 us
  waiting for transfers between devices  280 us (67%)
  local copies, waits for them, and re-layouts  56.7 us (13%)
  starting transfers between devices  34.6 us (8%)
  other arithmetic  16 us (4%)
  matrix products  15.1 us (4%)
  between operations  14.3 us (3%)
    unnamed x2, waiting for transfers between devices  86.4 us
    all_to_all x1, waiting for transfers between devices, body(): lax.all_to_all(input_grad, 'expert', split_axis=0, concat_axis=0, tiled=T...  54.2 us
    all_to_all x1, waiting for transfers between devices, body(): lax.all_to_all(sent_grads, 'expert', split_axis=0, concat_axis=0, tiled=T...  50.1 us
    all_to_all x1, waiting for transfers between devices, body(): lax.all_to_all(produced, 'expert', split_axis=0, concat_axis=0, tiled=True)  47 us
    all_to_all x1, waiting for transfers between devices, body(): lax.all_to_all(sent_rows, 'expert', split_axis=0, concat_axis=0, tiled=True)  42.6 us
    all_to_all x1, starting transfers between devices, body(): lax.all_to_all(sent_rows, 'expert', split_axis=0, concat_axis=0, tiled=True)  16.8 us
    unnamed x17, local copies, waits for them, and re-layouts  12.4 us
  transfers between devices with their start and end apart: 5, of which 5 were waited for; matrix products, arithmetic and copies ran while one was open for 12% of the time, Pallas kernels for 0%

commit v1 on v0

v1 whole, which is shorter than its diff:
```python
import functools

import jax
import jax.numpy as jnp
from jax import lax
from jax.experimental import pallas as pl
from jax.experimental.pallas import tpu as pltpu
from jax.sharding import PartitionSpec as P

BF = jnp.bfloat16
F32 = jnp.float32
MESH = pl.DeviceIdType.MESH
NX, NY = 4, 8
LANES = 256
CHUNK = 256
VMEM = pl.BlockSpec(memory_space=pltpu.VMEM)
ANY = pl.BlockSpec(memory_space=pl.ANY)


def put(wide, j, pieces, value):
    rows = value.shape[0]
    for h in range(2):
        wide[h][pl.ds(j, rows, stride=pieces), :] = value[:, h * 128 : (h + 1) * 128]


def take(wide, j, pieces, rows):
    return jnp.concatenate([wide[h][pl.ds(j, rows, stride=pieces), :] for h in range(2)], axis=1)


def fill(wide, value):
    for h in range(2):
        wide[h][...] = value[:, h * 128 : (h + 1) * 128]


def whole(wide):
    return jnp.concatenate([wide[0][...], wide[1][...]], axis=1)


def dot(a, b, ca, cb):
    return lax.dot_general(a, b, (((ca,), (cb,)), ((), ())), preferred_element_type=F32)


def one_hots(routes, experts, cap):
    top, tokens = routes.shape
    ids = lax.broadcasted_iota(jnp.int32, (experts, tokens), 0)
    chosen = [(routes[k : k + 1, :] == ids).astype(F32) for k in range(top)]
    before = (
        lax.broadcasted_iota(jnp.int32, (tokens, tokens), 0)
        < lax.broadcasted_iota(jnp.int32, (tokens, tokens), 1)
    ).astype(F32)
    counts = dot(sum(chosen).astype(BF), before.astype(BF), 1, 0)
    slots = lax.broadcasted_iota(jnp.int32, (experts * cap, tokens), 0)
    hots = []
    for k in range(top):
        position = jnp.sum(chosen[k] * counts, axis=0, keepdims=True)
        slot = routes[k : k + 1, :] * cap + position.astype(jnp.int32)
        hots.append((slots == slot).astype(F32))
    return hots


def route_weights(scores):
    e = jnp.exp(scores)
    return e / jnp.sum(e, axis=0, keepdims=True)


def pre_kernel(experts, cap, routes_ref, scores_ref, tokens_ref, grads_ref, x_ref, g_ref, *wide):
    hot0, hot1 = one_hots(routes_ref[...], experts, cap)
    w = route_weights(scores_ref[...])
    slot_w = jnp.sum(hot0 * w[0:1, :] + hot1 * w[1:2, :], axis=1, keepdims=True)
    hot = (hot0 + hot1).astype(BF)
    slots = experts * cap
    pieces = tokens_ref.shape[1] // LANES
    for src, dst, scale in ((tokens_ref, x_ref, None), (grads_ref, g_ref, slot_w)):
        for j in range(pieces):
            part = dot(hot, src[:, j * LANES : (j + 1) * LANES], 1, 0)
            if scale is not None:
                part = part * scale
            put(wide, j, pieces, part)
        dst[...] = whole(wide).astype(BF)


def post_kernel(experts, cap, routes_ref, scores_ref, out_ref, grad_ref, mixed_ref, token_ref, *wide):
    hot0, hot1 = one_hots(routes_ref[...], experts, cap)
    w = route_weights(scores_ref[...])
    tokens = w.shape[1]
    cols = jnp.transpose(jnp.concatenate([w, jnp.zeros((6, tokens), F32)], axis=0))
    w0, w1 = cols[:, 0:1], cols[:, 1:2]
    both = (hot0 + hot1).astype(BF)
    hot0, hot1 = hot0.astype(BF), hot1.astype(BF)
    slots = experts * cap
    pieces = mixed_ref.shape[1] // LANES
    fill(wide, out_ref[...].astype(F32))
    for j in range(pieces):
        part = take(wide, j, pieces, slots).astype(BF)
        mixed_ref[:, j * LANES : (j + 1) * LANES] = (
            w0 * dot(hot0, part, 0, 0) + w1 * dot(hot1, part, 0, 0)
        ).astype(BF)
    fill(wide, grad_ref[...].astype(F32))
    for j in range(pieces):
        part = take(wide, j, pieces, slots).astype(BF)
        token_ref[:, j * LANES : (j + 1) * LANES] = dot(both, part, 0, 0).astype(BF)


def expert_kernel(
    experts, cap, sx, sg, win_hbm, wout_hbm, rp, rg2, ggu, gd,
    win, wout, rx, rg, wide0, wide1, x, g, pre, hid, pg, s2p, s2g,
    ga, ra, y1, ry, gb, rb, x1, rx2,
    wsem, lsem, xs, xr, gs, gr, ps, pr, qs, qr, as_, ar, ys, yr, bs, br, cs, cr,
):
    wide = (wide0, wide1)
    me = lax.axis_index("expert")
    dp = lax.axis_index("dp")
    mx, my = dp // NY, lax.rem(dp, NY)
    n = experts
    slots = experts * cap
    width = x.shape[1]
    pieces = width // LANES
    hidden = hid.shape[1]
    n_in = 2 * hidden // CHUNK
    n_x = ga.shape[0]

    def zdev(k):
        return {"expert": lax.rem(me + k, n)}

    def xdev(d):
        return {"dp": lax.rem(mx + d, NX) * NY + my}

    def ydev(d):
        return {"dp": mx * NY + lax.rem(my + d, NY)}

    def remote(src, dst, ssem, rsem, dev):
        return pltpu.make_async_remote_copy(
            src_ref=src, dst_ref=dst, send_sem=ssem, recv_sem=rsem, device_id=dev, device_id_type=MESH
        )

    barrier = pltpu.get_barrier_semaphore()

    @pl.loop(1, n)
    def _(k):
        pl.semaphore_signal(barrier, inc=1, device_id=zdev(k), device_id_type=MESH)

    for d in range(1, NX):
        pl.semaphore_signal(barrier, inc=1, device_id=xdev(d), device_id_type=MESH)
    for d in range(1, NY):
        pl.semaphore_signal(barrier, inc=1, device_id=ydev(d), device_id_type=MESH)
    pl.semaphore_wait(barrier, (n - 1) + (NX - 1) + (NY - 1))

    def dispatch(k, src, dst, ssem, rsem):
        return remote(src.at[lax.rem(me + k, n)], dst.at[k], ssem.at[k], rsem.at[k], zdev(k))

    def give_back(k, src, dst, ssem, rsem):
        return remote(src.at[k], dst.at[me], ssem.at[k], rsem.at[k], zdev(n - k))

    def start_all(make, *refs):
        @pl.loop(1, n // 2)
        def _(k):
            make(k, *refs).start()
            make(n - k, *refs).start()

        make(n // 2, *refs).start()

    def wait_sent(make, *refs):
        @pl.loop(1, n)
        def _(k):
            make(k, *refs).wait_send()

    start_all(dispatch, sx, rx, xs, xr)
    start_all(dispatch, sg, rg, gs, gr)
    own_x = pltpu.make_async_copy(sx.at[me], rx.at[0], lsem.at[0])
    own_g = pltpu.make_async_copy(sg.at[me], rg.at[0], lsem.at[1])
    own_x.start()
    own_g.start()
    load_in = pltpu.make_async_copy(win_hbm, win, wsem.at[0])
    load_out = pltpu.make_async_copy(wout_hbm, wout, wsem.at[1])
    load_in.start()
    load_out.start()

    def narrow(src, dst):
        fill(wide, src[...].reshape(slots * pieces, LANES).astype(F32))
        for j in range(pieces):
            dst[:, j * LANES : (j + 1) * LANES] = take(wide, j, pieces, slots).astype(BF)

    def widen(rows, weights, dst):
        for j in range(pieces):
            put(wide, j, pieces, dot(rows, weights[j * LANES : (j + 1) * LANES, :], 1, 1))
        dst[...] = whole(wide).astype(BF).reshape(n, cap * pieces, LANES)

    own_x.wait()
    load_in.wait()
    load_out.wait()

    @pl.loop(1, n)
    def _(k):
        dispatch(k, sx, rx, xs, xr).wait_recv()

    narrow(rx, x)

    for c in range(hidden // CHUNK):
        lo, hi = c * CHUNK, (c + 1) * CHUNK
        gate = dot(x[...], win[:, lo:hi], 1, 0)
        up = dot(x[...], win[:, hidden + lo : hidden + hi], 1, 0)
        pre[:, lo:hi] = gate
        pre[:, hidden + lo : hidden + hi] = up
        hid[:, lo:hi] = (gate * (1.0 / (1.0 + jnp.exp(-gate))) * up).astype(BF)
    widen(hid[...], wout, s2p)
    start_all(give_back, s2p, rp, ps, pr)
    home_p = pltpu.make_async_copy(s2p.at[0], rp.at[me], lsem.at[0])
    home_p.start()

    own_g.wait()

    @pl.loop(1, n)
    def _(k):
        dispatch(k, sg, rg, gs, gr).wait_recv()

    narrow(rg, g)
    for c in range(hidden // CHUNK):
        lo, hi = c * CHUNK, (c + 1) * CHUNK
        hg = dot(g[...], wout[:, lo:hi], 1, 0)
        gate = pre[:, lo:hi]
        up = pre[:, hidden + lo : hidden + hi]
        s = 1.0 / (1.0 + jnp.exp(-gate))
        pg[:, lo:hi] = (hg * up * s * (1.0 + gate * (1.0 - s))).astype(BF)
        pg[:, hidden + lo : hidden + hi] = (hg * gate * s).astype(BF)

    rows_x = width // NX
    rows_y = rows_x // NY

    def send_a(c, d):
        return remote(
            ga.at[c, lax.rem(mx + d, NX)], ra.at[c, d], as_.at[c, d], ar.at[c, d], xdev(d)
        )

    def send_b(d):
        return remote(gb.at[:, lax.rem(my + d, NY)], rb.at[d], bs.at[d], br.at[d], ydev(d))

    def send_y(c, d):
        return remote(y1.at[c, lax.rem(my + d, NY)], ry.at[c, d], ys.at[c, d], yr.at[c, d], ydev(d))

    def send_c(d):
        return remote(x1.at[lax.rem(mx + d, NX)], rx2.at[d], cs.at[d], cr.at[d], xdev(d))

    last = hidden - CHUNK
    gb[...] = dot(g[...], hid[:, last:hidden], 0, 0).astype(BF).reshape(NX, NY, rows_y, CHUNK)
    for d in (1, 7, 2, 6, 3, 5, 4):
        send_b(d).start()
    for c in range(n_x):
        lo = c * CHUNK
        if c < n_in:
            part = dot(x[...], pg[:, lo : lo + CHUNK], 0, 0)
        else:
            lo -= n_in * CHUNK
            part = dot(g[...], hid[:, lo : lo + CHUNK], 0, 0)
        ga[c] = part.astype(BF).reshape(NX, rows_x, CHUNK)
        for d in (1, 3, 2):
            send_a(c, d).start()

    widen(pg[...], win, s2g)
    start_all(give_back, s2g, rg2, qs, qr)
    home_g = pltpu.make_async_copy(s2g.at[0], rg2.at[me], lsem.at[1])
    home_g.start()

    def sum_x(c):
        for d in range(1, NX):
            send_a(c, d).wait_recv()
        total = ga[c, mx].astype(F32)
        for d in range(1, NX):
            total = total + ra[c, d].astype(F32)
        y1[c] = total.astype(BF).reshape(NY, rows_y, CHUNK)
        for d in (1, 7, 2, 6, 3, 5, 4):
            send_y(c, d).start()

    def sum_y():
        for d in range(1, NY):
            send_b(d).wait_recv()
        total = gb[:, my].astype(F32)
        for d in range(1, NY):
            total = total + rb[d].astype(F32)
        x1[...] = total.astype(BF)
        for d in (1, 3, 2):
            send_c(d).start()

    for c in range(n_x):
        sum_x(c)
        if c == 1:
            sum_y()

    groups = float(NX * NY)
    for c in range(n_x):
        for d in range(1, NY):
            send_y(c, d).wait_recv()
        total = y1[c, my].astype(F32)
        for d in range(1, NY):
            total = total + ry[c, d].astype(F32)
        lo = c * CHUNK
        if c < n_in:
            ggu[:, lo : lo + CHUNK] = total / groups
        else:
            lo -= n_in * CHUNK
            gd[:, lo : lo + CHUNK] = total / groups
    for d in range(1, NX):
        send_c(d).wait_recv()
    total = x1[mx].astype(F32)
    for d in range(1, NX):
        total = total + rx2[d].astype(F32)
    gd[:, last:hidden] = total / groups

    home_p.wait()
    home_g.wait()

    @pl.loop(1, n)
    def _(k):
        give_back(k, s2p, rp, ps, pr).wait_recv()
        give_back(k, s2g, rg2, qs, qr).wait_recv()

    wait_sent(dispatch, sx, rx, xs, xr)
    wait_sent(dispatch, sg, rg, gs, gr)
    wait_sent(give_back, s2p, rp, ps, pr)
    wait_sent(give_back, s2g, rg2, qs, qr)
    for d in range(1, NX):
        for c in range(n_x):
            send_a(c, d).wait_send()
        send_c(d).wait_send()
    for d in range(1, NY):
        for c in range(n_x):
            send_y(c, d).wait_send()
        send_b(d).wait_send()


def body(tokens, routes, route_scores, out_grad, gate_up, down_weight):
    n = lax.axis_size("expert")
    rows, width = tokens.shape
    top = routes.shape[1]
    hidden = down_weight.shape[2]
    cap = (rows * top + n - 1) // n
    slots = n * cap
    pieces = width // LANES
    dma = pltpu.SemaphoreType.DMA
    vm = pltpu.VMEM
    routes_t, scores_t = routes.T, route_scores.T
    wire = jax.ShapeDtypeStruct((slots * pieces, LANES), BF)
    sx, sg = pl.pallas_call(
        functools.partial(pre_kernel, n, cap),
        out_shape=(wire, wire),
        in_specs=[VMEM] * 4,
        out_specs=(VMEM, VMEM),
        scratch_shapes=[vm((slots * pieces, 128), F32)] * 2,
        name="pack",
    )(routes_t, scores_t, tokens, out_grad)
    block = (n, cap * pieces, LANES)
    share = width // (NX * NY)
    n_x = 3 * hidden // CHUNK - 1
    rows_x = width // NX
    rp, rg, ggu, gd = pl.pallas_call(
        functools.partial(expert_kernel, n, cap),
        out_shape=(
            jax.ShapeDtypeStruct(block, BF),
            jax.ShapeDtypeStruct(block, BF),
            jax.ShapeDtypeStruct((share, 2 * hidden), F32),
            jax.ShapeDtypeStruct((share, hidden), F32),
        ),
        in_specs=[ANY] * 4,
        out_specs=(ANY, ANY, VMEM, VMEM),
        scratch_shapes=[
            vm((width, 2 * hidden), BF), vm((width, hidden), BF),
            vm(block, BF), vm(block, BF),
            vm((slots * pieces, 128), F32), vm((slots * pieces, 128), F32),
            vm((slots, width), BF), vm((slots, width), BF),
            vm((slots, 2 * hidden), F32), vm((slots, hidden), BF), vm((slots, 2 * hidden), BF),
            vm(block, BF), vm(block, BF),
            vm((n_x, NX, rows_x, CHUNK), BF), vm((n_x, NX, rows_x, CHUNK), BF),
            vm((n_x, NY, share, CHUNK), BF), vm((n_x, NY, share, CHUNK), BF),
            vm((NX, NY, share, CHUNK), BF), vm((NY, NX, share, CHUNK), BF),
            vm((NX, share, CHUNK), BF), vm((NX, share, CHUNK), BF),
            dma((2,)), dma((2,)),
            dma((n,)), dma((n,)), dma((n,)), dma((n,)), dma((n,)), dma((n,)), dma((n,)), dma((n,)),
            dma((n_x, NX)), dma((n_x, NX)), dma((n_x, NY)), dma((n_x, NY)),
            dma((NY,)), dma((NY,)), dma((NX,)), dma((NX,)),
        ],
        compiler_params=pltpu.CompilerParams(
            collective_id=0, has_side_effects=True, vmem_limit_bytes=56 << 20
        ),
        name="experts",
    )(sx.reshape(block), sg.reshape(block), gate_up[0], down_weight[0])
    outs = jax.ShapeDtypeStruct((rows, width), BF)
    mixed, token_grad = pl.pallas_call(
        functools.partial(post_kernel, n, cap),
        out_shape=(outs, outs),
        in_specs=[VMEM] * 4,
        out_specs=(VMEM, VMEM),
        scratch_shapes=[vm((slots * pieces, 128), F32)] * 2,
        name="combine",
    )(routes_t, scores_t, rp.reshape(slots * pieces, LANES), rg.reshape(slots * pieces, LANES))
    return mixed, token_grad, ggu[None], gd[None]


def solution(mesh):
    in_specs = (
        P(("dp", "expert"), None),
        P(("dp", "expert"), None),
        P(("dp", "expert"), None),
        P(("dp", "expert"), None),
        P("expert", None, None),
        P("expert", None, None),
    )
    out_specs = (
        P(("dp", "expert"), None),
        P(("dp", "expert"), None),
        P("expert", "dp", None),
        P("expert", "dp", None),
    )
    return jax.shard_map(body, mesh=mesh, in_specs=in_specs, out_specs=out_specs, check_vma=False)
```

time: 421 us -> 176 us (0.42)
  the two profiles are of different devices: /device:TPU:1 before, /device:TPU:64 now
where the time goes in v1:
time: 176 us
  Pallas kernels  174 us (99%)
    pallas_call x1, Pallas kernels, body(): pl.pallas_call(functools.partial(expert_kernel, n, cap), out_shape=(jax.S...  167 us
    pallas_call x1, Pallas kernels, body(): pl.pallas_call(functools.partial(post_kernel, n, cap), out_shape=(outs, o...  4.23 us

profile of v1, /device:TPU:64, one launch (start us, length us, event | category | flops | bytes accessed | tf_op | source)
XLA Modules:
  0.0 176.3 jit_solution(8654920106179303166)
XLA Ops:
  0.6 3.5 %pack.1 = (bf16[2112,256]{1,0:T(8,128)(2,1)}, bf16[2112,256]{1,0:T(8,128)(2,1)}) custom-call(s32[2,128]{1,0:T(2,128)} %bitcast.18, f32[2,128]{1,0:T(2,128)} %bitcast.20, bf16[128,2048]{1,0:T(8,128)(2,1)} %tokens_ref.1, bf16[128,2048]{1,0:T(8,128)(2,1)} %grads_ref.1), custom_call_target="tpu_custom_call" | custom-call | tf_op jit(solution)/shard_map/pack/pallas_call | solution.py:342
  4.1 166.5 %experts.1 = (bf16[24,88,256]{2,1,0:T(8,128)(2,1)}, bf16[24,88,256]{2,1,0:T(8,128)(2,1)}, f32[64,1024]{1,0:T(8,128)}, f32[64,512]{1,0:T(8,128)}) custom-call(bf16[24,88,256]{2,1,0:T(8,128)(2,1)} %bitcast.14, bf16[24,88,256]{2,1,0:T(8,128)(2,1)} %bitcast.15, bf16[2048,1024]{1,0:T(8,128)(2,1)} %bitcast.10, bf16[2048,512]{1,0:T(8,128)(2,1)} %bitcast.11), custom_call_target="tpu_custom_call" | custom-call | tf_op jit(solution)/shard_map/experts/pallas_call | solution.py:354
  170.7 0.0 copy-start
  170.7 0.0 copy-start.1
  170.7 4.2 %combine.1 = (bf16[128,2048]{1,0:T(8,128)(2,1)}, bf16[128,2048]{1,0:T(8,128)(2,1)}) custom-call(s32[2,128]{1,0:T(2,128)} %bitcast.19, f32[2,128]{1,0:T(2,128)} %bitcast.21, bf16[2112,256]{1,0:T(8,128)(2,1)} %bitcast.12, bf16[2112,256]{1,0:T(8,128)(2,1)} %bitcast.13), custom_call_target="tpu_custom_call" | custom-call | tf_op jit(solution)/shard_map/combine/pallas_call | solution.py:386
  174.9 0.0 copy-done
  174.9 0.7 copy.12
  175.6 0.0 copy-done.1
  175.6 0.7 copy.13
Async XLA Ops:
  170.7 4.2 %copy-start = (f32[64,1024]{1,0:T(8,128)S(1)}, f32[64,1024]{1,0:T(8,128)}, u32[]{:S(2)}) copy-start(f32[64,1024]{1,0:T(8,128)} %get-tuple-element.18) | copy-start | bytes 786436
  170.7 4.9 %copy-start.1 = (f32[64,512]{1,0:T(8,128)S(1)}, f32[64,512]{1,0:T(8,128)}, u32[]{:S(2)}) copy-start(f32[64,512]{1,0:T(8,128)} %get-tuple-element.19) | copy-start | bytes 393220

commit v2 on v1

--- a/solution.py
+++ b/solution.py
@@ -40,7 +40,7 @@
     return lax.dot_general(a, b, (((ca,), (cb,)), ((), ())), preferred_element_type=F32)
 
 
-def one_hots(routes, experts, cap):
+def slots_of(routes, experts, cap):
     top, tokens = routes.shape
     ids = lax.broadcasted_iota(jnp.int32, (experts, tokens), 0)
     chosen = [(routes[k : k + 1, :] == ids).astype(F32) for k in range(top)]
@@ -49,13 +49,10 @@
         < lax.broadcasted_iota(jnp.int32, (tokens, tokens), 1)
     ).astype(F32)
     counts = dot(sum(chosen).astype(BF), before.astype(BF), 1, 0)
-    slots = lax.broadcasted_iota(jnp.int32, (experts * cap, tokens), 0)
-    hots = []
-    for k in range(top):
-        position = jnp.sum(chosen[k] * counts, axis=0, keepdims=True)
-        slot = routes[k : k + 1, :] * cap + position.astype(jnp.int32)
-        hots.append((slots == slot).astype(F32))
-    return hots
+    return [
+        routes[k : k + 1, :].astype(F32) * cap + jnp.sum(chosen[k] * counts, axis=0, keepdims=True)
+        for k in range(top)
+    ]
 
 
 def route_weights(scores):
@@ -63,47 +60,24 @@
     return e / jnp.sum(e, axis=0, keepdims=True)
 
 
-def pre_kernel(experts, cap, routes_ref, scores_ref, tokens_ref, grads_ref, x_ref, g_ref, *wide):
-    hot0, hot1 = one_hots(routes_ref[...], experts, cap)
-    w = route_weights(scores_ref[...])
-    slot_w = jnp.sum(hot0 * w[0:1, :] + hot1 * w[1:2, :], axis=1, keepdims=True)
-    hot = (hot0 + hot1).astype(BF)
-    slots = experts * cap
-    pieces = tokens_ref.shape[1] // LANES
-    for src, dst, scale in ((tokens_ref, x_ref, None), (grads_ref, g_ref, slot_w)):
-        for j in range(pieces):
-            part = dot(hot, src[:, j * LANES : (j + 1) * LANES], 1, 0)
-            if scale is not None:
-                part = part * scale
-            put(wide, j, pieces, part)
-        dst[...] = whole(wide).astype(BF)
-
-
-def post_kernel(experts, cap, routes_ref, scores_ref, out_ref, grad_ref, mixed_ref, token_ref, *wide):
-    hot0, hot1 = one_hots(routes_ref[...], experts, cap)
-    w = route_weights(scores_ref[...])
-    tokens = w.shape[1]
-    cols = jnp.transpose(jnp.concatenate([w, jnp.zeros((6, tokens), F32)], axis=0))
-    w0, w1 = cols[:, 0:1], cols[:, 1:2]
-    both = (hot0 + hot1).astype(BF)
-    hot0, hot1 = hot0.astype(BF), hot1.astype(BF)
-    slots = experts * cap
-    pieces = mixed_ref.shape[1] // LANES
-    fill(wide, out_ref[...].astype(F32))
-    for j in range(pieces):
-        part = take(wide, j, pieces, slots).astype(BF)
-        mixed_ref[:, j * LANES : (j + 1) * LANES] = (
-            w0 * dot(hot0, part, 0, 0) + w1 * dot(hot1, part, 0, 0)
-        ).astype(BF)
+def token_kernel(slots, cols_ref, grad_ref, mixed_in, ggu_in, gd_in, mixed_ref, token_ref, ggu, gd, *wide):
+    tokens, width = token_ref.shape
+    pieces = width // LANES
+    ids = lax.broadcasted_iota(jnp.int32, (tokens, slots), 1).astype(F32)
+    cols = cols_ref[...]
+    both = ((ids == cols[:, 2:3]) | (ids == cols[:, 3:4])).astype(F32).astype(BF)
     fill(wide, grad_ref[...].astype(F32))
     for j in range(pieces):
         part = take(wide, j, pieces, slots).astype(BF)
-        token_ref[:, j * LANES : (j + 1) * LANES] = dot(both, part, 0, 0).astype(BF)
+        token_ref[:, j * LANES : (j + 1) * LANES] = dot(both, part, 1, 0).astype(BF)
+    mixed_ref[...] = mixed_in[...]
+    ggu[...] = ggu_in[...]
+    gd[...] = gd_in[...]
 
 
 def expert_kernel(
-    experts, cap, sx, sg, win_hbm, wout_hbm, rp, rg2, ggu, gd,
-    win, wout, rx, rg, wide0, wide1, x, g, pre, hid, pg, s2p, s2g,
+    experts, cap, routes_ref, scores_ref, tokens_ref, grads_ref, win_hbm, wout_hbm, rg2, mixed, ggu, gd, cols,
+    sx, sg, rp, win, wout, rx, rg, wide0, wide1, x, g, pre, hid, pg, s2p, s2g,
     ga, ra, y1, ry, gb, rb, x1, rx2,
     wsem, lsem, xs, xr, gs, gr, ps, pr, qs, qr, as_, ar, ys, yr, bs, br, cs, cr,
 ):
@@ -143,8 +117,6 @@
         pl.semaphore_signal(barrier, inc=1, device_id=xdev(d), device_id_type=MESH)
     for d in range(1, NY):
         pl.semaphore_signal(barrier, inc=1, device_id=ydev(d), device_id_type=MESH)
-    pl.semaphore_wait(barrier, (n - 1) + (NX - 1) + (NY - 1))
-
     def dispatch(k, src, dst, ssem, rsem):
         return remote(src.at[lax.rem(me + k, n)], dst.at[k], ssem.at[k], rsem.at[k], zdev(k))
 
@@ -164,16 +136,34 @@
         def _(k):
             make(k, *refs).wait_send()
 
-    start_all(dispatch, sx, rx, xs, xr)
-    start_all(dispatch, sg, rg, gs, gr)
     own_x = pltpu.make_async_copy(sx.at[me], rx.at[0], lsem.at[0])
     own_g = pltpu.make_async_copy(sg.at[me], rg.at[0], lsem.at[1])
-    own_x.start()
-    own_g.start()
     load_in = pltpu.make_async_copy(win_hbm, win, wsem.at[0])
     load_out = pltpu.make_async_copy(wout_hbm, wout, wsem.at[1])
     load_in.start()
     load_out.start()
+
+    slot0, slot1 = slots_of(routes_ref[...], n, cap)
+    w = route_weights(scores_ref[...])
+    ids = lax.broadcasted_iota(jnp.int32, (slots, w.shape[1]), 0).astype(F32)
+    hot0, hot1 = (ids == slot0).astype(F32), (ids == slot1).astype(F32)
+    slot_w = jnp.sum(hot0 * w[0:1, :] + hot1 * w[1:2, :], axis=1, keepdims=True)
+    hot = (hot0 + hot1).astype(BF)
+    cols[...] = jnp.transpose(jnp.concatenate([w, slot0, slot1, jnp.zeros((4, w.shape[1]), F32)], axis=0))
+
+    def pack(src, dst, scale):
+        for j in range(pieces):
+            part = dot(hot, src[:, j * LANES : (j + 1) * LANES], 1, 0)
+            put(wide, j, pieces, part if scale is None else part * scale)
+        dst[...] = whole(wide).astype(BF).reshape(n, cap * pieces, LANES)
+
+    pack(tokens_ref, sx, None)
+    own_x.start()
+    pl.semaphore_wait(barrier, (n - 1) + (NX - 1) + (NY - 1))
+    start_all(dispatch, sx, rx, xs, xr)
+    pack(grads_ref, sg, slot_w)
+    own_g.start()
+    start_all(dispatch, sg, rg, gs, gr)
 
     def narrow(src, dst):
         fill(wide, src[...].reshape(slots * pieces, LANES).astype(F32))
@@ -241,10 +231,8 @@
         return remote(x1.at[lax.rem(mx + d, NX)], rx2.at[d], cs.at[d], cr.at[d], xdev(d))
 
     last = hidden - CHUNK
-    gb[...] = dot(g[...], hid[:, last:hidden], 0, 0).astype(BF).reshape(NX, NY, rows_y, CHUNK)
-    for d in (1, 7, 2, 6, 3, 5, 4):
-        send_b(d).start()
-    for c in range(n_x):
+
+    def piece_x(c):
         lo = c * CHUNK
         if c < n_in:
             part = dot(x[...], pg[:, lo : lo + CHUNK], 0, 0)
@@ -255,6 +243,13 @@
         for d in (1, 3, 2):
             send_a(c, d).start()
 
+    piece_x(0)
+    gb[...] = dot(g[...], hid[:, last:hidden], 0, 0).astype(BF).reshape(NX, NY, rows_y, CHUNK)
+    for d in (1, 7, 2, 6, 3, 5, 4):
+        send_b(d).start()
+    for c in range(1, n_x):
+        piece_x(c)
+
     widen(pg[...], win, s2g)
     start_all(give_back, s2g, rg2, qs, qr)
     home_g = pltpu.make_async_copy(s2g.at[0], rg2.at[me], lsem.at[1])
@@ -280,10 +275,30 @@
         for d in (1, 3, 2):
             send_c(d).start()
 
+    def mix():
+        home_p.wait()
+
+        @pl.loop(1, n)
+        def _(k):
+            give_back(k, s2p, rp, ps, pr).wait_recv()
+
+        mine = cols[...]
+        tokens = mine.shape[0]
+        at = lax.broadcasted_iota(jnp.int32, (tokens, slots), 1).astype(F32)
+        first = (at == mine[:, 2:3]).astype(F32).astype(BF)
+        second = (at == mine[:, 3:4]).astype(F32).astype(BF)
+        fill(wide, rp[...].reshape(slots * pieces, LANES).astype(F32))
+        for j in range(pieces):
+            part = take(wide, j, pieces, slots).astype(BF)
+            mixed[:, j * LANES : (j + 1) * LANES] = (
+                mine[:, 0:1] * dot(first, part, 1, 0) + mine[:, 1:2] * dot(second, part, 1, 0)
+            ).astype(BF)
+
     for c in range(n_x):
         sum_x(c)
         if c == 1:
             sum_y()
+            mix()
 
     groups = float(NX * NY)
     for c in range(n_x):
@@ -305,12 +320,10 @@
         total = total + rx2[d].astype(F32)
     gd[:, last:hidden] = total / groups
 
-    home_p.wait()
     home_g.wait()
 
     @pl.loop(1, n)
     def _(k):
-        give_back(k, s2p, rp, ps, pr).wait_recv()
         give_back(k, s2g, rg2, qs, qr).wait_recv()
 
     wait_sent(dispatch, sx, rx, xs, xr)
@@ -337,31 +350,27 @@
     pieces = width // LANES
     dma = pltpu.SemaphoreType.DMA
     vm = pltpu.VMEM
-    routes_t, scores_t = routes.T, route_scores.T
-    wire = jax.ShapeDtypeStruct((slots * pieces, LANES), BF)
-    sx, sg = pl.pallas_call(
-        functools.partial(pre_kernel, n, cap),
-        out_shape=(wire, wire),
-        in_specs=[VMEM] * 4,
-        out_specs=(VMEM, VMEM),
-        scratch_shapes=[vm((slots * pieces, 128), F32)] * 2,
-        name="pack",
-    )(routes_t, scores_t, tokens, out_grad)
     block = (n, cap * pieces, LANES)
     share = width // (NX * NY)
     n_x = 3 * hidden // CHUNK - 1
     rows_x = width // NX
-    rp, rg, ggu, gd = pl.pallas_call(
+    outs = jax.ShapeDtypeStruct((rows, width), BF)
+    shares = (
+        jax.ShapeDtypeStruct((share, 2 * hidden), F32),
+        jax.ShapeDtypeStruct((share, hidden), F32),
+    )
+    rg, mixed, ggu, gd, cols = pl.pallas_call(
         functools.partial(expert_kernel, n, cap),
         out_shape=(
             jax.ShapeDtypeStruct(block, BF),
-            jax.ShapeDtypeStruct(block, BF),
-            jax.ShapeDtypeStruct((share, 2 * hidden), F32),
-            jax.ShapeDtypeStruct((share, hidden), F32),
+            outs,
+            *shares,
+            jax.ShapeDtypeStruct((rows, 8), F32),
         ),
-        in_specs=[ANY] * 4,
-        out_specs=(ANY, ANY, VMEM, VMEM),
+        in_specs=[VMEM] * 4 + [ANY] * 2,
+        out_specs=(ANY, VMEM, VMEM, VMEM, VMEM),
         scratch_shapes=[
+            vm(block, BF), vm(block, BF), vm(block, BF),
             vm((width, 2 * hidden), BF), vm((width, hidden), BF),
             vm(block, BF), vm(block, BF),
             vm((slots * pieces, 128), F32), vm((slots * pieces, 128), F32),
@@ -381,16 +390,15 @@
             collective_id=0, has_side_effects=True, vmem_limit_bytes=56 << 20
         ),
         name="experts",
-    )(sx.reshape(block), sg.reshape(block), gate_up[0], down_weight[0])
-    outs = jax.ShapeDtypeStruct((rows, width), BF)
-    mixed, token_grad = pl.pallas_call(
-        functools.partial(post_kernel, n, cap),
-        out_shape=(outs, outs),
-        in_specs=[VMEM] * 4,
-        out_specs=(VMEM, VMEM),
+    )(routes.T, route_scores.T, tokens, out_grad, gate_up[0], down_weight[0])
+    mixed, token_grad, ggu, gd = pl.pallas_call(
+        functools.partial(token_kernel, slots),
+        out_shape=(outs, outs, *shares),
+        in_specs=[VMEM] * 5,
+        out_specs=(VMEM,) * 4,
         scratch_shapes=[vm((slots * pieces, 128), F32)] * 2,
-        name="combine",
-    )(routes_t, scores_t, rp.reshape(slots * pieces, LANES), rg.reshape(slots * pieces, LANES))
+        name="token",
+    )(cols, rg.reshape(slots * pieces, LANES), mixed, ggu, gd)
     return mixed, token_grad, ggu[None], gd[None]
 
 

time: 176 us -> 170 us (0.966)
  Pallas kernels: 174 us -> 169 us
    pallas_call x2 -> x1, Pallas kernels: 7.71 us -> 3.22 us  [body(): pl.pallas_call(functools.partial(token_kernel, slots), out_shape=(outs, o...]
where the time goes in v2:
time: 170 us
  Pallas kernels  169 us (99%)
    pallas_call x1, Pallas kernels, body(): pl.pallas_call(functools.partial(expert_kernel, n, cap), out_shape=(jax.S...  166 us

profile of v2, /device:TPU:64, one launch (start us, length us, event | category | flops | bytes accessed | tf_op | source)
XLA Modules:
  0.0 169.9 jit_solution(14948572229278710146)
XLA Ops:
  0.6 166.1 %experts.1 = (bf16[24,88,256]{2,1,0:T(8,128)(2,1)}, bf16[128,2048]{1,0:T(8,128)(2,1)}, f32[64,1024]{1,0:T(8,128)}, f32[64,512]{1,0:T(8,128)}, f32[128,8]{1,0:T(8,128)}) custom-call(s32[2,128]{1,0:T(2,128)} %bitcast.10, f32[2,128]{1,0:T(2,128)} %bitcast.11, bf16[128,2048]{1,0:T(8,128)(2,1)} %tokens_ref.1, bf16[128,2048]{1,0:T(8,128)(2,1)} %grads_ref.1, ...), custom_call_target="tpu_custom_call" | custom-call | tf_op jit(solution)/shard_map/experts/pallas_call | solution.py:362
  166.7 3.2 %token_.1 = (bf16[128,2048]{1,0:T(8,128)(2,1)}, bf16[128,2048]{1,0:T(8,128)(2,1)}, f32[64,1024]{1,0:T(8,128)}, f32[64,512]{1,0:T(8,128)}) custom-call(f32[128,8]{1,0:T(8,128)} %get-tuple-element.13.cols_ref, bf16[2112,256]{1,0:T(8,128)(2,1)} %bitcast.9, bf16[128,2048]{1,0:T(8,128)(2,1)} %get-tuple-element.15.mixed_in, f32[64,1024]{1,0:T(8,128)} %get-tuple-element.16.ggu_in, ...), custom_call_target="tpu_custom_call" | custom-call | tf_op jit(solution)/shard_map/token/pallas_call | solution.py:394

commit v3 on v2

--- a/solution.py
+++ b/solution.py
@@ -76,10 +76,10 @@
 
 
 def expert_kernel(
-    experts, cap, routes_ref, scores_ref, tokens_ref, grads_ref, win_hbm, wout_hbm, rg2, mixed, ggu, gd, cols,
-    sx, sg, rp, win, wout, rx, rg, wide0, wide1, x, g, pre, hid, pg, s2p, s2g,
-    ga, ra, y1, ry, gb, rb, x1, rx2,
-    wsem, lsem, xs, xr, gs, gr, ps, pr, qs, qr, as_, ar, ys, yr, bs, br, cs, cr,
+    experts, cap, routes_hbm, scores_hbm, tokens_hbm, grads_hbm, win_hbm, wout_hbm, rg2, mixed_hbm, ggu_hbm, gd_hbm, cols_hbm,
+    routes_ref, scores_ref, tokens_ref, grads_ref, mixed, ggu, gd, cols, isem, osem, sx, sg, rp, win, wout, rx, rg, wide0, wide1, x, g, pre, hid, pg, s2p, s2g,
+    ga, ra, y1, ry, gb, rb, x1, rx2, rh,
+    hs, hr, wsem, lsem, xs, xr, gs, gr, ps, pr, qs, qr, as_, ar, ys, yr, bs, br, cs, cr,
 ):
     wide = (wide0, wide1)
     me = lax.axis_index("expert")
@@ -107,6 +107,20 @@
             src_ref=src, dst_ref=dst, send_sem=ssem, recv_sem=rsem, device_id=dev, device_id_type=MESH
         )
 
+    loads = [
+        pltpu.make_async_copy(src, dst, isem.at[i])
+        for i, (src, dst) in enumerate(
+            (
+                (routes_hbm, routes_ref),
+                (scores_hbm, scores_ref),
+                (tokens_hbm, tokens_ref),
+                (grads_hbm, grads_ref),
+            )
+        )
+    ]
+    for load in loads:
+        load.start()
+
     barrier = pltpu.get_barrier_semaphore()
 
     @pl.loop(1, n)
@@ -117,6 +131,7 @@
         pl.semaphore_signal(barrier, inc=1, device_id=xdev(d), device_id_type=MESH)
     for d in range(1, NY):
         pl.semaphore_signal(barrier, inc=1, device_id=ydev(d), device_id_type=MESH)
+
     def dispatch(k, src, dst, ssem, rsem):
         return remote(src.at[lax.rem(me + k, n)], dst.at[k], ssem.at[k], rsem.at[k], zdev(k))
 
@@ -143,6 +158,8 @@
     load_in.start()
     load_out.start()
 
+    loads[0].wait()
+    loads[1].wait()
     slot0, slot1 = slots_of(routes_ref[...], n, cap)
     w = route_weights(scores_ref[...])
     ids = lax.broadcasted_iota(jnp.int32, (slots, w.shape[1]), 0).astype(F32)
@@ -157,10 +174,12 @@
             put(wide, j, pieces, part if scale is None else part * scale)
         dst[...] = whole(wide).astype(BF).reshape(n, cap * pieces, LANES)
 
+    loads[2].wait()
     pack(tokens_ref, sx, None)
     own_x.start()
     pl.semaphore_wait(barrier, (n - 1) + (NX - 1) + (NY - 1))
     start_all(dispatch, sx, rx, xs, xr)
+    loads[3].wait()
     pack(grads_ref, sg, slot_w)
     own_g.start()
     start_all(dispatch, sg, rg, gs, gr)
@@ -174,6 +193,12 @@
         for j in range(pieces):
             put(wide, j, pieces, dot(rows, weights[j * LANES : (j + 1) * LANES, :], 1, 1))
         dst[...] = whole(wide).astype(BF).reshape(n, cap * pieces, LANES)
+
+    outs = [
+        pltpu.make_async_copy(src, dst, osem.at[i])
+        for i, (src, dst) in enumerate(((mixed, mixed_hbm), (ggu, ggu_hbm), (gd, gd_hbm), (cols, cols_hbm)))
+    ]
+    outs[3].start()
 
     own_x.wait()
     load_in.wait()
@@ -221,6 +246,22 @@
             ga.at[c, lax.rem(mx + d, NX)], ra.at[c, d], as_.at[c, d], ar.at[c, d], xdev(d)
         )
 
+    half = rows_x // 2
+    near = (1, NX - 1)
+
+    def send_h(c, d):
+        return remote(
+            ga.at[c, lax.rem(mx + 2, NX), pl.ds(d * half, half)], rh.at[c, d], hs.at[c, d], hr.at[c, d], xdev(near[d])
+        )
+
+    def relay(c):
+        for d in range(2):
+            send_h(c, d).wait_recv()
+            block = lax.rem(mx + near[d], NX)
+            rows = pl.ds(d * half, half)
+            ga[c, block, rows] = (ga[c, block, rows].astype(F32) + rh[c, d].astype(F32)).astype(BF)
+            send_a(c, near[d]).start()
+
     def send_b(d):
         return remote(gb.at[:, lax.rem(my + d, NY)], rb.at[d], bs.at[d], br.at[d], ydev(d))
 
@@ -240,15 +281,18 @@
             lo -= n_in * CHUNK
             part = dot(g[...], hid[:, lo : lo + CHUNK], 0, 0)
         ga[c] = part.astype(BF).reshape(NX, rows_x, CHUNK)
-        for d in (1, 3, 2):
-            send_a(c, d).start()
-
+        for d in range(2):
+            send_h(c, d).start()
+
+    early = 2
     piece_x(0)
     gb[...] = dot(g[...], hid[:, last:hidden], 0, 0).astype(BF).reshape(NX, NY, rows_y, CHUNK)
     for d in (1, 7, 2, 6, 3, 5, 4):
         send_b(d).start()
     for c in range(1, n_x):
         piece_x(c)
+        if c <= early:
+            relay(c - 1)
 
     widen(pg[...], win, s2g)
     start_all(give_back, s2g, rg2, qs, qr)
@@ -256,10 +300,10 @@
     home_g.start()
 
     def sum_x(c):
-        for d in range(1, NX):
+        for d in near:
             send_a(c, d).wait_recv()
         total = ga[c, mx].astype(F32)
-        for d in range(1, NX):
+        for d in near:
             total = total + ra[c, d].astype(F32)
         y1[c] = total.astype(BF).reshape(NY, rows_y, CHUNK)
         for d in (1, 7, 2, 6, 3, 5, 4):
@@ -294,11 +338,16 @@
                 mine[:, 0:1] * dot(first, part, 1, 0) + mine[:, 1:2] * dot(second, part, 1, 0)
             ).astype(BF)
 
+    for c in range(early, n_x - 1):
+        relay(c)
     for c in range(n_x):
         sum_x(c)
+        if c == 0:
+            relay(n_x - 1)
         if c == 1:
             sum_y()
             mix()
+            outs[0].start()
 
     groups = float(NX * NY)
     for c in range(n_x):
@@ -319,6 +368,8 @@
     for d in range(1, NX):
         total = total + rx2[d].astype(F32)
     gd[:, last:hidden] = total / groups
+    outs[1].start()
+    outs[2].start()
 
     home_g.wait()
 
@@ -326,14 +377,18 @@
     def _(k):
         give_back(k, s2g, rg2, qs, qr).wait_recv()
 
+    for out in outs:
+        out.wait()
     wait_sent(dispatch, sx, rx, xs, xr)
     wait_sent(dispatch, sg, rg, gs, gr)
     wait_sent(give_back, s2p, rp, ps, pr)
     wait_sent(give_back, s2g, rg2, qs, qr)
     for d in range(1, NX):
-        for c in range(n_x):
-            send_a(c, d).wait_send()
         send_c(d).wait_send()
+    for c in range(n_x):
+        for d in range(2):
+            send_h(c, d).wait_send()
+            send_a(c, near[d]).wait_send()
     for d in range(1, NY):
         for c in range(n_x):
             send_y(c, d).wait_send()
@@ -367,9 +422,12 @@
             *shares,
             jax.ShapeDtypeStruct((rows, 8), F32),
         ),
-        in_specs=[VMEM] * 4 + [ANY] * 2,
-        out_specs=(ANY, VMEM, VMEM, VMEM, VMEM),
+        in_specs=[ANY] * 6,
+        out_specs=(ANY,) * 5,
         scratch_shapes=[
+            vm((top, rows), jnp.int32), vm((top, rows), F32), vm((rows, width), BF), vm((rows, width), BF),
+            vm((rows, width), BF), vm((share, 2 * hidden), F32), vm((share, hidden), F32), vm((rows, 8), F32),
+            dma((4,)), dma((4,)),
             vm(block, BF), vm(block, BF), vm(block, BF),
             vm((width, 2 * hidden), BF), vm((width, hidden), BF),
             vm(block, BF), vm(block, BF),
@@ -381,6 +439,8 @@
             vm((n_x, NY, share, CHUNK), BF), vm((n_x, NY, share, CHUNK), BF),
             vm((NX, NY, share, CHUNK), BF), vm((NY, NX, share, CHUNK), BF),
             vm((NX, share, CHUNK), BF), vm((NX, share, CHUNK), BF),
+            vm((n_x, 2, rows_x // 2, CHUNK), BF),
+            dma((n_x, 2)), dma((n_x, 2)),
             dma((2,)), dma((2,)),
             dma((n,)), dma((n,)), dma((n,)), dma((n,)), dma((n,)), dma((n,)), dma((n,)), dma((n,)),
             dma((n_x, NX)), dma((n_x, NX)), dma((n_x, NY)), dma((n_x, NY)),

time: 170 us -> 166 us (0.976)
  the two profiles are of different devices: /device:TPU:64 before, /device:TPU:1 now
where the time goes in v3:
time: 166 us; the launch traced here: 163 us
  Pallas kernels  162 us (98%)
    pallas_call x1, Pallas kernels, body(): pl.pallas_call(functools.partial(expert_kernel, n, cap), out_shape=(jax.S...  159 us

profile of v3, /device:TPU:1, one launch (start us, length us, event | category | flops | bytes accessed | tf_op | source)
XLA Modules:
  0.0 163.1 jit_solution(15967595530186459054)
XLA Ops:
  0.6 159.3 %experts.1 = (bf16[24,88,256]{2,1,0:T(8,128)(2,1)}, bf16[128,2048]{1,0:T(8,128)(2,1)}, f32[64,1024]{1,0:T(8,128)}, f32[64,512]{1,0:T(8,128)}, f32[128,8]{1,0:T(8,128)}) custom-call(s32[2,128]{1,0:T(2,128)} %bitcast.10, f32[2,128]{1,0:T(2,128)} %bitcast.11, bf16[128,2048]{1,0:T(8,128)(2,1)} %tokens_hbm.1, bf16[128,2048]{1,0:T(8,128)(2,1)} %grads_hbm.1, ...), custom_call_target="tpu_custom_call" | custom-call | tf_op jit(solution)/shard_map/experts/pallas_call | solution.py:417
  159.9 3.2 %token_.1 = (bf16[128,2048]{1,0:T(8,128)(2,1)}, bf16[128,2048]{1,0:T(8,128)(2,1)}, f32[64,1024]{1,0:T(8,128)}, f32[64,512]{1,0:T(8,128)}) custom-call(f32[128,8]{1,0:T(8,128)} %get-tuple-element.13.cols_ref, bf16[2112,256]{1,0:T(8,128)(2,1)} %bitcast.9, bf16[128,2048]{1,0:T(8,128)(2,1)} %get-tuple-element.15.mixed_in, f32[64,1024]{1,0:T(8,128)} %get-tuple-element.16.ggu_in, ...), custom_call_target="tpu_custom_call" | custom-call | tf_op jit(solution)/shard_map/token/pallas_call | solution.py:454

commit v4 on v3

--- a/solution.py
+++ b/solution.py
@@ -132,8 +132,11 @@
     for d in range(1, NY):
         pl.semaphore_signal(barrier, inc=1, device_id=ydev(d), device_id_type=MESH)
 
+    third = n // 3
+    ahead = third // 2
+
     def dispatch(k, src, dst, ssem, rsem):
-        return remote(src.at[lax.rem(me + k, n)], dst.at[k], ssem.at[k], rsem.at[k], zdev(k))
+        return remote(src.at[lax.rem(k + ahead, n)], dst.at[k], ssem.at[k], rsem.at[k], zdev(k))
 
     def give_back(k, src, dst, ssem, rsem):
         return remote(src.at[k], dst.at[me], ssem.at[k], rsem.at[k], zdev(n - k))
@@ -151,8 +154,8 @@
         def _(k):
             make(k, *refs).wait_send()
 
-    own_x = pltpu.make_async_copy(sx.at[me], rx.at[0], lsem.at[0])
-    own_g = pltpu.make_async_copy(sg.at[me], rg.at[0], lsem.at[1])
+    own_x = pltpu.make_async_copy(sx.at[ahead], rx.at[0], lsem.at[0])
+    own_g = pltpu.make_async_copy(sg.at[ahead], rg.at[0], lsem.at[1])
     load_in = pltpu.make_async_copy(win_hbm, win, wsem.at[0])
     load_out = pltpu.make_async_copy(wout_hbm, wout, wsem.at[1])
     load_in.start()
@@ -163,24 +166,39 @@
     slot0, slot1 = slots_of(routes_ref[...], n, cap)
     w = route_weights(scores_ref[...])
     ids = lax.broadcasted_iota(jnp.int32, (slots, w.shape[1]), 0).astype(F32)
-    hot0, hot1 = (ids == slot0).astype(F32), (ids == slot1).astype(F32)
+    turn = (lax.rem(n - me + ahead, n) * cap).astype(F32)
+
+    def turned(slot):
+        slot = slot + turn
+        return jnp.where(slot >= slots, slot - slots, slot)
+
+    hot0, hot1 = (ids == turned(slot0)).astype(F32), (ids == turned(slot1)).astype(F32)
     slot_w = jnp.sum(hot0 * w[0:1, :] + hot1 * w[1:2, :], axis=1, keepdims=True)
-    hot = (hot0 + hot1).astype(BF)
+    hot = hot0 + hot1
     cols[...] = jnp.transpose(jnp.concatenate([w, slot0, slot1, jnp.zeros((4, w.shape[1]), F32)], axis=0))
 
-    def pack(src, dst, scale):
+    def pack(src, dst, scale, lo, blocks):
+        first, rows = lo * cap, blocks * cap
+        pick = hot[first : first + rows].astype(BF)
         for j in range(pieces):
-            part = dot(hot, src[:, j * LANES : (j + 1) * LANES], 1, 0)
-            put(wide, j, pieces, part if scale is None else part * scale)
-        dst[...] = whole(wide).astype(BF).reshape(n, cap * pieces, LANES)
+            part = dot(pick, src[:, j * LANES : (j + 1) * LANES], 1, 0)
+            put(wide, first * pieces + j, pieces, part if scale is None else part * scale)
+        wire = pl.ds(first * pieces, rows * pieces)
+        packed = jnp.concatenate([wide[h][wire, :] for h in range(2)], axis=1).astype(BF)
+        dst[lo : lo + blocks] = packed.reshape(blocks, cap * pieces, LANES)
 
     loads[2].wait()
-    pack(tokens_ref, sx, None)
+    pack(tokens_ref, sx, None, 0, third)
     own_x.start()
     pl.semaphore_wait(barrier, (n - 1) + (NX - 1) + (NY - 1))
-    start_all(dispatch, sx, rx, xs, xr)
+    for part in range(3):
+        if part:
+            pack(tokens_ref, sx, None, part * third, third)
+        away = [i - ahead for i in range(part * third, (part + 1) * third)]
+        for k in sorted((k for k in away if k), key=lambda k: min(k % n, -k % n)):
+            dispatch(k % n, sx, rx, xs, xr).start()
     loads[3].wait()
-    pack(grads_ref, sg, slot_w)
+    pack(grads_ref, sg, slot_w, 0, n)
     own_g.start()
     start_all(dispatch, sg, rg, gs, gr)
 
@@ -295,7 +313,13 @@
             relay(c - 1)
 
     widen(pg[...], win, s2g)
-    start_all(give_back, s2g, rg2, qs, qr)
+    give_back(n // 2, s2g, rg2, qs, qr).start()
+
+    @pl.loop(1, n // 2)
+    def _(k):
+        give_back(n // 2 - k, s2g, rg2, qs, qr).start()
+        give_back(n // 2 + k, s2g, rg2, qs, qr).start()
+
     home_g = pltpu.make_async_copy(s2g.at[0], rg2.at[me], lsem.at[1])
     home_g.start()
 

time: 166 us -> 168 us (1.012); the launches traced: 163 us -> 168 us
  Pallas kernels: 162 us -> 167 us
    pallas_call x1, Pallas kernels: 159 us -> 164 us  [body(): pl.pallas_call(functools.partial(expert_kernel, n, cap), out_shape=(jax.S...]
where the time goes in v4:
time: 168 us
  Pallas kernels  167 us (99%)
    pallas_call x1, Pallas kernels, body(): pl.pallas_call(functools.partial(expert_kernel, n, cap), out_shape=(jax.S...  164 us

profile of v4, /device:TPU:1, one launch (start us, length us, event | category | flops | bytes accessed | tf_op | source)
XLA Modules:
  0.0 167.5 jit_solution(14016157792547434388)
XLA Ops:
  0.6 163.7 %experts.1 = (bf16[24,88,256]{2,1,0:T(8,128)(2,1)}, bf16[128,2048]{1,0:T(8,128)(2,1)}, f32[64,1024]{1,0:T(8,128)}, f32[64,512]{1,0:T(8,128)}, f32[128,8]{1,0:T(8,128)}) custom-call(s32[2,128]{1,0:T(2,128)} %bitcast.10, f32[2,128]{1,0:T(2,128)} %bitcast.11, bf16[128,2048]{1,0:T(8,128)(2,1)} %tokens_hbm.1, bf16[128,2048]{1,0:T(8,128)(2,1)} %grads_hbm.1, ...), custom_call_target="tpu_custom_call" | custom-call | tf_op jit(solution)/shard_map/experts/pallas_call | solution.py:441
  164.3 3.2 %token_.1 = (bf16[128,2048]{1,0:T(8,128)(2,1)}, bf16[128,2048]{1,0:T(8,128)(2,1)}, f32[64,1024]{1,0:T(8,128)}, f32[64,512]{1,0:T(8,128)}) custom-call(f32[128,8]{1,0:T(8,128)} %get-tuple-element.13.cols_ref, bf16[2112,256]{1,0:T(8,128)(2,1)} %bitcast.9, bf16[128,2048]{1,0:T(8,128)(2,1)} %get-tuple-element.15.mixed_in, f32[64,1024]{1,0:T(8,128)} %get-tuple-element.16.ggu_in, ...), custom_call_target="tpu_custom_call" | custom-call | tf_op jit(solution)/shard_map/token/pallas_call | solution.py:478
